TPU v7x, 512 devices: a whole 4x4x16 slice. The times are simulated.
512 devices in a mesh: group: 16 (over z), shard: 32 (over y, x, core).
Axes of the slice: x: 4, y: 4, z: 16, core: 2. Of those that a mesh axis runs over, the one named last changes fastest.
Arguments:
- entry_grads: float32 [16, 32, 256, 1280], P('group', 'shard'), may hold values from -800 to 800
- exit_grads: float32 [16, 32, 256, 1024], P('group', 'shard'), may hold values from -800 to 800
- entry_params: float32 [32, 256, 1280], P('shard', 'group'), may hold values from -0.15625 to 0.15625
- exit_params: float32 [32, 256, 1024], P('shard', 'group'), may hold values from -0.15625 to 0.15625
- entry_mean: float32 [32, 256, 1280], P('shard', 'group'), may hold values from -1.5 to 1.5
- exit_mean: float32 [32, 256, 1024], P('shard', 'group'), may hold values from -1.5 to 1.5
- entry_square: float32 [32, 256, 1280], P('shard', 'group'), may hold values from 0.01 to 1
- exit_square: float32 [32, 256, 1024], P('shard', 'group'), may hold values from 0.01 to 1
Outputs:
- entry_master: float32 [32, 256, 1280], P('shard', 'group')
- exit_master: float32 [32, 256, 1024], P('shard', 'group')
- entry_moment: float32 [32, 256, 1280], P('shard', 'group')
- exit_moment: float32 [32, 256, 1024], P('shard', 'group')
- entry_variance: float32 [32, 256, 1280], P('shard', 'group')
- exit_variance: float32 [32, 256, 1024], P('shard', 'group')
- entry_weights: bfloat16 [32, 256, 1280], P('shard')
- exit_weights: bfloat16 [32, 256, 1024], P('shard')
All inputs are finite; a program needn't handle non-finite values.
Results may differ from a plain program's by a relative error of at most 0.0004.
Values may be sent and summed in bfloat16 or wider, within the bound.
No kernel may reach another device: no remote copies, remote signals or barrier semaphores. Data moves between devices by JAX's collectives and lax.ppermute only.
A program may use at most 64 MiB of HBM per device.

v0:
```python
import jax
import jax.numpy as jnp
from jax import lax
from jax.sharding import PartitionSpec as P

beta_first = 0.9
beta_second = 0.95
learn_rate = 0.01
decay_rate = 0.1
epsilon = 1e-08
correct_first = 1.0 - 0.9**40
correct_second = 1.0 - 0.95**40


def adamw_step(params, mean, square, total, clip):
    grads = clip * total
    moment = beta_first * mean + (1.0 - beta_first) * grads
    variance = beta_second * square + (1.0 - beta_second) * grads * grads
    update = moment / correct_first / (jnp.sqrt(variance / correct_second) + epsilon)
    master = params - learn_rate * (update + decay_rate * params)
    return (master, moment, variance)


def sum_everywhere(values):
    axes = ("group", "shard")
    lanes = jnp.sum(values.reshape(-1, 128), axis=0)
    sent = jnp.broadcast_to(lanes, (lax.axis_size(axes), 1, 128))
    return jnp.sum(lax.all_to_all(sent, axes, 0, 0))


def body(
    entry_grads,
    exit_grads,
    entry_params,
    exit_params,
    entry_mean,
    exit_mean,
    entry_square,
    exit_square,
):
    entry_rows_dev = entry_grads.shape[2]
    exit_rows_dev = exit_grads.shape[2]
    entry_width = entry_grads.shape[3]
    exit_width = exit_grads.shape[3]
    entry_local = entry_grads.reshape(entry_rows_dev, entry_width)
    exit_local = exit_grads.reshape(exit_rows_dev, exit_width)
    packed = jnp.concatenate([entry_local, exit_local], axis=1)
    total = lax.psum_scatter(packed, "group", scatter_dimension=0, tiled=True)
    entry_total = total[:, :entry_width]
    exit_total = total[:, entry_width:]
    squares = sum_everywhere(total * total)
    count = (entry_rows_dev * entry_width + exit_rows_dev * exit_width) * lax.axis_size("shard")
    limit = jnp.sqrt(jnp.float32(count))
    clip = jnp.minimum(jnp.float32(1.0), limit / (jnp.sqrt(squares) + 1e-06))
    entry_master, entry_moment, entry_variance = adamw_step(
        entry_params[0], entry_mean[0], entry_square[0], entry_total, clip
    )
    exit_master, exit_moment, exit_variance = adamw_step(
        exit_params[0], exit_mean[0], exit_square[0], exit_total, clip
    )
    entry_round = entry_master.astype(jnp.bfloat16)
    exit_round = exit_master.astype(jnp.bfloat16)
    entry_weights = lax.all_gather(entry_round, "group", axis=0, tiled=True)
    exit_weights = lax.all_gather(exit_round, "group", axis=0, tiled=True)
    return (
        entry_master[None],
        exit_master[None],
        entry_moment[None],
        exit_moment[None],
        entry_variance[None],
        exit_variance[None],
        entry_weights[None],
        exit_weights[None],
    )


def solution(mesh):
    placed = (
        P("group", "shard", None, None),
        P("group", "shard", None, None),
        P("shard", "group", None),
        P("shard", "group", None),
        P("shard", "group", None),
        P("shard", "group", None),
        P("shard", "group", None),
        P("shard", "group", None),
    )
    return jax.shard_map(
        body,
        mesh=mesh,
        in_specs=placed,
        out_specs=(
            P("shard", "group", None),
            P("shard", "group", None),
            P("shard", "group", None),
            P("shard", "group", None),
            P("shard", "group", None),
            P("shard", "group", None),
            P("shard", None, None),
            P("shard", None, None),
        ),
        check_vma=False,
    )
```

profile of v0, /device:TPU:2, one launch (start us, length us, event | category | flops | bytes accessed | tf_op | source)
XLA Modules:
  0.0 204.4 jit_solution(7940237761173604504)
XLA Ops:
  7.2 0.0 reduce-scatter.2.cloned.1.call-start
  7.2 3.2 %pad_maximum_fusion = f32[256,2304]{1,0:T(8,128)} fusion(f32[256,1024]{1,0:T(8,128)} %bitcast.67, f32[256,1280]{1,0:T(8,128)} %bitcast.65), kind=kLoop, calls=%fused_computation | loop fusion | flops 589824 | bytes 4718592 | tf_op jit(solution)/shard_map/concatenate | solution.py:47
  10.4 0.0 copy-start.4
  10.4 0.0 copy-start.5
  10.4 0.0 copy-start.6
  10.4 0.0 copy-start.1
  10.4 0.0 copy-start.2
  10.5 0.0 copy-start.3
  10.5 0.0 reduce-scatter.2.cloned.1.call-update
  10.5 78.5 %reduce-scatter.2.cloned.1.call-done = f32[16,2304]{1,0:T(8,128)} async-done(((f32[256,2304]{1,0:T(8,128)}), f32[16,2304]{1,0:T(8,128)}) %reduce-scatter.2.cloned.1.call-update) | async-done | bytes 147472 | tf_op jit(solution)/shard_map/reduce_scatter | solution.py:48
  89.0 0.0 copy-start
  89.0 1.1 mul.96
  90.1 0.1 reduce_sum.18
  90.2 0.1 broadcast_in_dim.27
  90.3 40.8 %all_to_all.5 = f32[512,1,128]{2,1,0:T(1,128)S(1)} all-to-all(f32[512,1,128]{2,1,0:T(1,128)S(1)} %broadcast_in_dim.27), channel_id=1, replica_groups=mesh['group'=16,'shard'=32] {'group','shard'}, dimensions={0} | all-to-all | bytes 524288 | tf_op jit(solution)/shard_map/all_to_all | solution.py:28
  131.1 0.7 reduce_sum.19
  132.5 0.0 copy-done.4
  132.5 0.0 copy-done.5
  132.5 0.0 copy-done.6
  132.5 1.5 fusion.10
  134.1 30.4 %all_gather.7 = bf16[256,1024]{1,0:T(8,128)(2,1)S(1)} all-gather(bf16[16,1024]{1,0:T(8,128)(2,1)S(1)} %get-tuple-element.8), channel_id=1, replica_groups=mesh['group'=16,'shard'=32] {'group'}, dimensions={0}, use_global_device_ids=true | all-gather | bytes 557056 | tf_op jit(solution)/shard_map/all_gather | solution.py:64
  164.5 0.0 copy-done.1
  164.5 0.0 copy-done.2
  164.5 0.0 copy-done.3
  164.5 0.0 copy-done
  164.5 0.7 fusion.11
  165.2 30.7 %all_gather.6 = bf16[256,1280]{1,0:T(8,128)(2,1)S(1)} all-gather(bf16[16,1280]{1,0:T(8,128)(2,1)S(1)} %get-tuple-element.10), channel_id=1, replica_groups=mesh['group'=16,'shard'=32] {'group'}, dimensions={0}, use_global_device_ids=true | all-gather | bytes 696320 | tf_op jit(solution)/shard_map/all_gather | solution.py:63
  195.9 0.8 copy.19
  196.8 0.8 copy.20
  (1 shorter events, 0.0 us)
Async XLA Ops:
  7.2 81.9 %reduce-scatter.2.cloned.1.call-start = ((), (), s32[]{:S(2)}) async-start(), calls=%async_computation.2 | async-start | bytes 2506752 | tf_op jit(solution)/shard_map/reduce_scatter | solution.py:48
  10.4 122.1 %copy-start.4 = (f32[1,16,1024]{2,1,0:T(8,128)S(1)}, f32[1,16,1024]{2,1,0:T(8,128)}, u32[]{:S(2)}) copy-start(f32[1,16,1024]{2,1,0:T(8,128)} %param.15) | copy-start | bytes 196612
  10.4 122.1 %copy-start.5 = (f32[1,16,1024]{2,1,0:T(8,128)S(1)}, f32[1,16,1024]{2,1,0:T(8,128)}, u32[]{:S(2)}) copy-start(f32[1,16,1024]{2,1,0:T(8,128)} %param.13) | copy-start | bytes 196612
  10.4 122.1 %copy-start.6 = (f32[1,16,1024]{2,1,0:T(8,128)S(1)}, f32[1,16,1024]{2,1,0:T(8,128)}, u32[]{:S(2)}) copy-start(f32[1,16,1024]{2,1,0:T(8,128)} %param.11) | copy-start | bytes 196612
  10.4 154.1 %copy-start.1 = (f32[1,16,1280]{2,1,0:T(8,128)S(1)}, f32[1,16,1280]{2,1,0:T(8,128)}, u32[]{:S(2)}) copy-start(f32[1,16,1280]{2,1,0:T(8,128)} %param.14) | copy-start | bytes 245764
  10.4 154.1 %copy-start.2 = (f32[1,16,1280]{2,1,0:T(8,128)S(1)}, f32[1,16,1280]{2,1,0:T(8,128)}, u32[]{:S(2)}) copy-start(f32[1,16,1280]{2,1,0:T(8,128)} %param.12) | copy-start | bytes 245764
  10.5 154.1 %copy-start.3 = (f32[1,16,1280]{2,1,0:T(8,128)S(1)}, f32[1,16,1280]{2,1,0:T(8,128)}, u32[]{:S(2)}) copy-start(f32[1,16,1280]{2,1,0:T(8,128)} %param.10) | copy-start | bytes 245764
  89.0 75.5 %copy-start = (f32[16,2304]{1,0:T(8,128)S(1)}, f32[16,2304]{1,0:T(8,128)}, u32[]{:S(2)}) copy-start(f32[16,2304]{1,0:T(8,128)} %reduce-scatter.2.cloned.1.call-done) | copy-start | bytes 442372
Sparse Core Ops, SparseCore 0:
  10.8 78.1 reduce-scatter.1
where the time goes:
time: 205 us; the launch traced here: 204 us
  blocking collectives  102 us (50%)
  waiting for transfers between devices  78.6 us (38%)
  between operations  14.8 us (7%)
  other arithmetic  7.27 us (4%)
    reduce_scatter x1, waiting for transfers between devices, body(): total = lax.psum_scatter(packed, 'group', scatter_dimension=0, tiled=True)  78.5 us
    all_to_all x1, blocking collectives, sum_everywhere(): return jnp.sum(lax.all_to_all(sent, axes, 0, 0))  40.8 us
    all_gather x1, blocking collectives, body(): entry_weights = lax.all_gather(entry_round, 'group', axis=0, tiled=True)  30.7 us
    all_gather x1, blocking collectives, body(): exit_weights = lax.all_gather(exit_round, 'group', axis=0, tiled=True)  30.4 us
  transfers between devices with their start and end apart: 1, of which 1 were waited for; matrix products, arithmetic and copies ran while one was open for 0% of the time, Pallas kernels for 0%

commit v1 on v0

--- a/solution.py
+++ b/solution.py
@@ -10,6 +10,15 @@
 epsilon = 1e-08
 correct_first = 1.0 - 0.9**40
 correct_second = 1.0 - 0.95**40
+
+
+def recover_strips_all(patch, m):
+    next_value = jnp.split(
+        lax.all_gather(jnp.concatenate([patch, m], axis=1), "group", axis=0, tiled=True),
+        [patch.shape[1]],
+        axis=1,
+    )
+    return next_value
 
 
 def adamw_step(params, mean, square, total, clip):
@@ -60,8 +69,7 @@
     )
     entry_round = entry_master.astype(jnp.bfloat16)
     exit_round = exit_master.astype(jnp.bfloat16)
-    entry_weights = lax.all_gather(entry_round, "group", axis=0, tiled=True)
-    exit_weights = lax.all_gather(exit_round, "group", axis=0, tiled=True)
+    entry_weights, exit_weights = recover_strips_all(entry_round, exit_round)
     return (
         entry_master[None],
         exit_master[None],

time: 205 us -> 207 us (level)
  waiting for transfers between devices: 78.6 us -> 140 us
  blocking collectives: 102 us -> 40.8 us
  local copies, waits for them, and re-layouts: 1.81 us -> 4.02 us
    all_gather x0 -> x1, waiting for transfers between devices: none -> 61.2 us  [recover_strips_all(): lax.all_gather(jnp.concatenate([patch, m], axis=1), 'group', axis=0, tile...]
    all_gather x2 -> x0, blocking collectives: 61.1 us -> none  [the longest x1 30.7 us: body(): entry_weights = lax.all_gather(entry_round, 'group', axis=0, tiled=True)]
    broadcast_in_dim x0 -> x2, local copies, waits for them, and re-layouts: none -> 3.83 us  [the longest x1 1.96 us: body(): entry_weights[None]]
  transfers between devices with their start and end apart: 1 -> 2, of which waited for: 1 -> 2; matrix products, arithmetic and copies ran while one was open for 0% -> 0% of each run, Pallas kernels for 0% -> 0%
where the time goes in v1:
time: 207 us
  waiting for transfers between devices  140 us (68%)
  blocking collectives  40.8 us (20%)
  between operations  14.9 us (7%)
  other arithmetic  7.05 us (3%)
  local copies, waits for them, and re-layouts  4.02 us (2%)
    reduce_scatter x1, waiting for transfers between devices, body(): total = lax.psum_scatter(packed, 'group', scatter_dimension=0, tiled=True)  78.5 us
    all_gather x1, waiting for transfers between devices, recover_strips_all(): lax.all_gather(jnp.concatenate([patch, m], axis=1), 'group', axis=0, tile...  61.2 us
    all_to_all x1, blocking collectives, sum_everywhere(): return jnp.sum(lax.all_to_all(sent, axes, 0, 0))  40.8 us
  transfers between devices with their start and end apart: 2, of which 2 were waited for; matrix products, arithmetic and copies ran while one was open for 0% of the time, Pallas kernels for 0%

profile of v1, /device:TPU:2, one launch (start us, length us, event | category | flops | bytes accessed | tf_op | source)
XLA Modules:
  0.0 206.5 jit_solution(15535089711261778054)
XLA Ops:
  7.2 0.0 reduce-scatter.2.cloned.1.call-start
  7.2 3.2 %pad_maximum_fusion = f32[256,2304]{1,0:T(8,128)} fusion(f32[256,1024]{1,0:T(8,128)} %bitcast.67, f32[256,1280]{1,0:T(8,128)} %bitcast.65), kind=kLoop, calls=%fused_computation | loop fusion | flops 589824 | bytes 4718592 | tf_op jit(solution)/shard_map/concatenate | solution.py:56
  10.4 0.0 reduce-scatter.2.cloned.1.call-update
  10.4 0.0 copy-start.4
  10.4 0.0 copy-start.5
  10.5 0.0 copy-start.6
  10.5 0.0 copy-start.1
  10.5 0.0 copy-start.2
  10.5 0.0 copy-start.3
  10.5 0.0 all-gather.2.cloned.1.call-start
  10.6 78.5 %reduce-scatter.2.cloned.1.call-done = f32[16,2304]{1,0:T(8,128)} async-done(((f32[256,2304]{1,0:T(8,128)}), f32[16,2304]{1,0:T(8,128)}) %reduce-scatter.2.cloned.1.call-update) | async-done | bytes 147472 | tf_op jit(solution)/shard_map/reduce_scatter | solution.py:57
  89.0 0.0 copy-start
  89.0 1.1 mul.96
  90.1 0.1 reduce_sum.18
  90.2 0.1 broadcast_in_dim.27
  90.3 40.8 %all_to_all.5 = f32[512,1,128]{2,1,0:T(1,128)S(1)} all-to-all(f32[512,1,128]{2,1,0:T(1,128)S(1)} %broadcast_in_dim.27), channel_id=1, replica_groups=mesh['group'=16,'shard'=32] {'group','shard'}, dimensions={0} | all-to-all | bytes 524288 | tf_op jit(solution)/shard_map/all_to_all | solution.py:37
  131.1 0.7 reduce_sum.19
  132.5 0.0 copy-done.4
  132.5 0.0 copy-done.5
  132.5 0.0 copy-done.6
  132.5 0.0 copy-done
  132.6 0.7 fusion.11
  133.3 0.0 copy-done.1
  133.3 0.0 copy-done.2
  133.3 0.0 copy-done.3
  133.3 0.7 fusion.10
  134.0 0.6 pad_maximum_fusion.1
  134.6 0.0 all-gather.2.cloned.1.call-update
  134.7 61.2 %all-gather.2.cloned.1.call-done = bf16[256,2304]{1,0:T(8,128)(2,1)} async-done(((bf16[16,2304]{1,0:T(8,128)(2,1)}), bf16[256,2304]{1,0:T(8,128)(2,1)}) %all-gather.2.cloned.1.call-update) | async-done | bytes 1179664 | tf_op jit(solution)/shard_map/all_gather | solution.py:17
  195.8 1.9 slice_bitcast_fusion.1
  197.7 2.0 slice_bitcast_fusion
  (1 shorter events, 0.0 us)
Async XLA Ops:
  7.2 81.9 %reduce-scatter.2.cloned.1.call-start = ((), (), s32[]{:S(2)}) async-start(), calls=%async_computation.2 | async-start | bytes 2506752 | tf_op jit(solution)/shard_map/reduce_scatter | solution.py:57
  10.4 122.1 %copy-start.4 = (f32[1,16,1024]{2,1,0:T(8,128)S(1)}, f32[1,16,1024]{2,1,0:T(8,128)}, u32[]{:S(2)}) copy-start(f32[1,16,1024]{2,1,0:T(8,128)} %param.15) | copy-start | bytes 196612
  10.4 122.1 %copy-start.5 = (f32[1,16,1024]{2,1,0:T(8,128)S(1)}, f32[1,16,1024]{2,1,0:T(8,128)}, u32[]{:S(2)}) copy-start(f32[1,16,1024]{2,1,0:T(8,128)} %param.13) | copy-start | bytes 196612
  10.5 122.1 %copy-start.6 = (f32[1,16,1024]{2,1,0:T(8,128)S(1)}, f32[1,16,1024]{2,1,0:T(8,128)}, u32[]{:S(2)}) copy-start(f32[1,16,1024]{2,1,0:T(8,128)} %param.11) | copy-start | bytes 196612
  10.5 122.8 %copy-start.1 = (f32[1,16,1280]{2,1,0:T(8,128)S(1)}, f32[1,16,1280]{2,1,0:T(8,128)}, u32[]{:S(2)}) copy-start(f32[1,16,1280]{2,1,0:T(8,128)} %param.14) | copy-start | bytes 245764
  10.5 122.8 %copy-start.2 = (f32[1,16,1280]{2,1,0:T(8,128)S(1)}, f32[1,16,1280]{2,1,0:T(8,128)}, u32[]{:S(2)}) copy-start(f32[1,16,1280]{2,1,0:T(8,128)} %param.12) | copy-start | bytes 245764
  10.5 122.8 %copy-start.3 = (f32[1,16,1280]{2,1,0:T(8,128)S(1)}, f32[1,16,1280]{2,1,0:T(8,128)}, u32[]{:S(2)}) copy-start(f32[1,16,1280]{2,1,0:T(8,128)} %param.10) | copy-start | bytes 245764
  10.5 185.3 %all-gather.2.cloned.1.call-start = ((), (), s32[]{:S(2)}) async-start(), calls=%async_computation.3 | async-start | bytes 1253376 | tf_op jit(solution)/shard_map/all_gather | solution.py:17
  89.0 43.5 %copy-start = (f32[16,2304]{1,0:T(8,128)S(1)}, f32[16,2304]{1,0:T(8,128)}, u32[]{:S(2)}) copy-start(f32[16,2304]{1,0:T(8,128)} %reduce-scatter.2.cloned.1.call-done) | copy-start | bytes 442372
Sparse Core Ops, SparseCore 0:
  10.8 78.1 reduce-scatter.1
  134.8 61.0 all-gather.1
